TPU v7x, 128 devices: a whole 4x4x4 slice. The times are simulated.
128 devices in a mesh: wide: 16 (over x_lo, y, core), narrow: 8 (over z, x_hi).
Axes of the slice: x: 4 (x_hi: 2, x_lo: 2; x = x_hi * 2 + x_lo), y: 4, z: 4, core: 2. Of those that a mesh axis runs over, the one named last changes fastest.
Arguments:
- tokens: bfloat16 [4096, 2048], P('wide', 'narrow'), may hold values from -6 to 6
- norm_gain: bfloat16 [2048], replicated, may hold values from 0.25 to 1.75
- router: bfloat16 [2048, 8], replicated, may hold values from -0.125 to 0.125
- routes: int32 [4096, 2], P('wide'), may hold values from 0 to 7, all different within a row
- kv_weight: bfloat16 [4096, 2048], P('narrow', 'wide'), may hold values from -0.125 to 0.125
- query_weight: bfloat16 [16384, 2048], P('narrow', 'wide'), may hold values from -0.125 to 0.125
- out_weight: bfloat16 [16384, 2048], P('narrow', 'wide'), may hold values from -0.09375 to 0.09375
- prefix_cache: bfloat16 [12288, 4096], P('wide', 'narrow'), may hold values from -225 to 225
- suffix_lengths: int32 [4], replicated, may hold values from 1 to 3328, 4096 in all
- prefix_lengths: int32 [4], replicated, may hold values from 1 to 6144, 12288 in all
Outputs:
- mixed: bfloat16 [4096, 2048], P('wide', 'narrow')
Inputs may be any that keep to these rules, and one draw needn't show every extreme that they name: `routes`: each token names 2 different experts. `suffix_lengths`: they sum to 4096. `prefix_lengths`: they sum to 12288.
All inputs are finite; a program needn't handle non-finite values.
Results may differ from a plain program's by a relative error of at most 0.012.
The roundings to bfloat16 on the way count: a program that leaves them out, or rounds other values in their place, can miss the bound.
Values may be sent and summed in bfloat16 or wider, within the bound.
No kernel may reach another device: no remote copies, remote signals or barrier semaphores. Data moves between devices by JAX's collectives and lax.ppermute only.
A program may use at most 320 MiB of HBM per device.

v0:
```python
import math
import jax
import jax.numpy as jnp
from jax import lax
from jax.sharding import PartitionSpec as P

H = 128
E = 8
eps = 1e-06
floor_value = -1e30


def tenant_of(positions, lengths):
    bounds = jnp.cumsum(lengths)
    return jnp.sum((positions[:, None] >= bounds[None, :]).astype(jnp.int32), axis=1)


def attend(carried, queries, key_block, value_block, allowed, scaling):
    highest, totals, summed = carried
    scores = (
        jnp.einsum("hrd,nhd->hrn", queries, key_block, preferred_element_type=jnp.float32) * scaling
    )
    scores = jnp.where(allowed[None, :, :], scores, -jnp.inf)
    new_highest = jnp.maximum(highest, jnp.max(scores, axis=2))
    weights = jnp.exp(scores - new_highest[:, :, None])
    factor = jnp.exp(highest - new_highest)
    totals = totals * factor + jnp.sum(weights, axis=2)
    summed = summed * factor[:, :, None] + jnp.einsum(
        "hrn,nhd->hrd",
        weights,
        value_block.astype(jnp.float32),
        precision=lax.Precision.HIGHEST,
        preferred_element_type=jnp.float32,
    )
    return (new_highest, totals, summed)


def over_blocks(
    carried, queries, cache_rows, row_tenant, row_index, key_tenant, key_index, scaling, causal
):
    length = cache_rows.shape[0]
    block_size = math.gcd(length, 512)
    steps_count = length // block_size
    cache_blocks = cache_rows.reshape((steps_count, block_size) + cache_rows.shape[1:])
    tenant_blocks = key_tenant.reshape(steps_count, block_size)
    index_blocks = key_index.reshape(steps_count, block_size)

    def advance(current, inputs):
        rows_here, tenant_here, index_here = inputs
        allowed = row_tenant[:, None] == tenant_here[None, :]
        if causal:
            allowed = allowed & (index_here[None, :] <= row_index[:, None])
        return (
            attend(
                current, queries, rows_here[:, :, 0, :], rows_here[:, :, 1, :], allowed, scaling
            ),
            None,
        )

    carried, unused = lax.scan(advance, carried, (cache_blocks, tenant_blocks, index_blocks))
    return carried


def on_device(
    tokens,
    norm_gain,
    router,
    routes,
    kv_weight,
    query_weight,
    out_weight,
    prefix_cache,
    suffix_lengths,
    prefix_lengths,
):
    whole = lax.all_gather(tokens, "narrow", axis=1, tiled=True)
    tok_rows = whole.shape[0]
    local_heads = kv_weight.shape[0] // (2 * H)
    slot_count = routes.shape[1]
    scaling = H ** (-0.5)
    floats = whole.astype(jnp.float32)
    normed = (
        floats
        * lax.rsqrt(jnp.mean(floats * floats, axis=1, keepdims=True) + eps)
        * norm_gain.astype(jnp.float32)
    ).astype(jnp.bfloat16)
    logits = jnp.dot(normed, router, preferred_element_type=jnp.float32)
    one_hot = routes[:, :, None] == jnp.arange(E, dtype=jnp.int32)[None, None, :]
    chosen = jnp.sum(jnp.where(one_hot, logits[:, None, :], 0.0), axis=2)
    gate_values = jax.nn.softmax(chosen, axis=1)
    choose = one_hot.astype(jnp.bfloat16)
    kv_part = lax.dot_general(
        normed,
        lax.all_gather(kv_weight, "wide", axis=1, tiled=True),
        (((1,), (1,)), ((), ())),
        preferred_element_type=jnp.float32,
    )
    query_part = lax.dot_general(
        normed,
        lax.all_gather(query_weight, "wide", axis=1, tiled=True),
        (((1,), (1,)), ((), ())),
        preferred_element_type=jnp.float32,
    )
    kv_local = kv_part.astype(jnp.bfloat16).reshape(tok_rows, local_heads, 2, H)
    query_all = query_part.astype(jnp.bfloat16).reshape(tok_rows, local_heads, E, H)
    selected = jnp.einsum(
        "tje,thed->htjd", choose, query_all, preferred_element_type=jnp.float32
    ).astype(jnp.bfloat16)
    row_count = tok_rows * slot_count
    queries = selected.reshape(local_heads, row_count, H)
    first_token = lax.axis_index("wide") * tok_rows
    token_index = first_token + jnp.arange(tok_rows, dtype=jnp.int32)
    row_index = jnp.repeat(token_index, slot_count)
    row_tenant = tenant_of(row_index, suffix_lengths)
    start_carry = (
        jnp.full((local_heads, row_count), floor_value, jnp.float32),
        jnp.zeros((local_heads, row_count), jnp.float32),
        jnp.zeros((local_heads, row_count, H), jnp.float32),
    )
    shard_piece = lax.all_gather(prefix_cache, "wide", axis=0, tiled=True)
    piece_rows = shard_piece.shape[0]
    slot_index = jnp.arange(piece_rows, dtype=jnp.int32)
    slot_tenant = tenant_of(slot_index, prefix_lengths)
    cache_rows = shard_piece.reshape(piece_rows, local_heads, 2, H)
    carried = over_blocks(
        start_carry,
        queries,
        cache_rows,
        row_tenant,
        row_index,
        slot_tenant,
        slot_index,
        scaling,
        False,
    )
    shard_piece = lax.all_gather(kv_local, "wide", axis=0, tiled=True)
    piece_rows = shard_piece.shape[0]
    key_index = jnp.arange(piece_rows, dtype=jnp.int32)
    key_tenant = tenant_of(key_index, suffix_lengths)
    carried = over_blocks(
        carried, queries, shard_piece, row_tenant, row_index, key_tenant, key_index, scaling, True
    )
    highest, totals, summed = carried
    attended = (summed / totals[:, :, None]).reshape(local_heads, tok_rows, slot_count, H)
    weighted = (attended * gate_values[None, :, :, None]).astype(jnp.bfloat16)
    padded = (
        jnp.einsum("tje,htjd->thed", choose, weighted, preferred_element_type=jnp.float32)
        .astype(jnp.bfloat16)
        .reshape(tok_rows, local_heads * E * H)
    )
    partial_out = jnp.dot(
        padded,
        lax.all_gather(out_weight, "wide", axis=1, tiled=True),
        preferred_element_type=jnp.float32,
    )
    return lax.psum_scatter(partial_out, "narrow", scatter_dimension=1, tiled=True).astype(
        jnp.bfloat16
    )


def solution(mesh):
    placed = (
        P("wide", "narrow"),
        P(),
        P(),
        P("wide", None),
        P("narrow", "wide"),
        P("narrow", "wide"),
        P("narrow", "wide"),
        P("wide", "narrow"),
        P(),
        P(),
    )
    return jax.shard_map(
        on_device, mesh=mesh, in_specs=placed, out_specs=P("wide", "narrow"), check_vma=False
    )
```

profile of v0, /device:TPU:0, one launch (start us, length us, event | category | flops | bytes accessed | tf_op | source)
XLA Modules:
  0.0 498.0 jit_solution(3596680702898717761)
XLA Ops:
  10.1 47.4 %all-gather.9.cloned.1.call-done = bf16[256,2048]{1,0:T(8,128)(2,1)} async-done(((bf16[256,256]{1,0:T(8,128)(2,1)}), bf16[256,2048]{1,0:T(8,128)(2,1)}) %all-gather.9.cloned.1.call-update) | async-done | bytes 1048592 | tf_op jit(solution)/shard_map/all_gather | solution.py:76
  59.0 35.4 %all-gather.13.cloned.1.call-done = bf16[512,2048]{1,0:T(8,128)(2,1)} async-done(((bf16[512,128]{1,0:T(8,128)(2,1)}), bf16[512,2048]{1,0:T(8,128)(2,1)}) %all-gather.13.cloned.1.call-update) | async-done | bytes 2097168 | tf_op jit(solution)/shard_map/all_gather | solution.py:94
  94.4 2.7 convolution_convert_fusion.2
  101.9 55.0 %all-gather.11.cloned.1.call-done = bf16[2048,2048]{1,0:T(8,128)(2,1)} async-done(((bf16[2048,128]{1,0:T(8,128)(2,1)}), bf16[2048,2048]{1,0:T(8,128)(2,1)}) %all-gather.11.cloned.1.call-update) | async-done | bytes 8388624 | tf_op jit(solution)/shard_map/all_gather | solution.py:100
  157.0 5.8 %fusion.15 = bf16[32,8,16,128]{3,1,2,0:T(8,128)(2,1)S(1)} fusion(bf16[2048,2048]{1,0:T(8,128)(2,1)} %all-gather.11.cloned.1.call-done, bf16[256,2048]{1,0:T(8,128)(2,1)S(1)} %copy-done.1, f32[2048]{0:T(1024)S(1)} %convert_element_type.48, f32[256]{0:T(256)S(1)} %add_rsqrt_fusion), kind=kOutput, calls=%fused_computation.41 | convolution fusion | flops 2150105088 | bytes 10494976 | tf_op jit(solution)/shard_map/dot_general | solution.py:98
  164.4 65.7 %all-gather.7.cloned.1.call-done = bf16[12288,512]{1,0:T(8,128)(2,1)} async-done(((bf16[768,512]{1,0:T(8,128)(2,1)}), bf16[12288,512]{1,0:T(8,128)(2,1)}) %all-gather.7.cloned.1.call-update) | async-done | bytes 12582928 | tf_op jit(solution)/shard_map/all_gather | solution.py:120
  230.1 18.2 %reshape.233 = bf16[24,512,2,2,128]{4,3,2,1,0:T(2,128)(2,1)} reshape(bf16[12288,512]{1,0:T(8,128)(2,1)} %all-gather.7.cloned.1.call-done) | data formatting | bytes 25165824 | tf_op jit(solution)/shard_map/reshape;reshape | solution.py:44
  248.3 112.6 %while.31 = (s32[]{:T(128)}, f32[2,512]{1,0:T(2,128)S(1)}, f32[2,512]{1,0:T(2,128)S(1)}, f32[2,512,128]{2,1,0:T(8,128)S(1)}, s32[512]{0:T(512)S(1)}, /*index=5*/...) while((s32[]{:T(128)}, f32[2,512]{1,0:T(2,128)S(1)}, ...), condition=%wide.region_8.9_spmd.clone, body=%wide.region_5.8_spmd.clone.sunk | while | flops 943330304 | bytes 11870357 | solution.py:60
  251.0 2.0 fusion.61
  255.7 2.0 fusion.61
  260.4 2.0 fusion.61
  265.1 2.0 fusion.61
  269.8 2.0 fusion.61
  274.5 2.0 fusion.61
  279.1 2.0 fusion.61
  283.8 2.0 fusion.61
  288.5 2.0 fusion.61
  293.2 2.0 fusion.61
  297.9 2.0 fusion.61
  302.6 2.0 fusion.61
  307.4 2.0 fusion.61
  312.0 2.0 fusion.61
  316.7 2.0 fusion.61
  321.4 2.0 fusion.61
  326.1 2.0 fusion.61
  330.8 2.0 fusion.61
  340.2 2.0 fusion.61
  349.6 2.0 fusion.61
  358.9 2.0 fusion.61
  361.0 43.5 %while.30 = (s32[]{:T(128)}, f32[2,512]{1,0:T(2,128)S(1)}, f32[2,512]{1,0:T(2,128)S(1)}, f32[2,512,128]{2,1,0:T(8,128)S(1)}, s32[512]{0:T(512)S(1)}, /*index=5*/...) while((s32[]{:T(128)}, f32[2,512]{1,0:T(2,128)S(1)}, ...), condition=%wide.region_13.14_spmd.clone, body=%wide.region_10.13_spmd.clone.sunk | while | flops 943720448 | bytes 9789041 | solution.py:60
  406.1 7.1 %fusion.17 = f32[256,2048]{1,0:T(8,128)} fusion(bf16[2048,2048]{1,0:T(8,128)(2,1)} %all-gather.17.cloned.1.call-done, bf16[32,8,16,128]{3,2,1,0:T(8,128)(2,1)S(1)} %bitcast.97), kind=kOutput, calls=%fused_computation.45 | convolution fusion | flops 2147483648 | bytes 11534336 | tf_op jit(solution)/shard_map/dot_general | solution.py:151
  413.2 76.3 %reduce-scatter.2.cloned.1.call-done = f32[256,256]{1,0:T(8,128)} async-done(((f32[256,2048]{1,0:T(8,128)}), f32[256,256]{1,0:T(8,128)}) %reduce-scatter.2.cloned.1.call-update) | async-done | bytes 262160 | tf_op jit(solution)/shard_map/reduce_scatter | solution.py:156
  (412 shorter events, 126.8 us)
Async XLA Ops:
  6.5 93.3 %copy-start = (bf16[2048,8]{0,1:T(8,128)(2,1)S(1)}, bf16[2048,8]{0,1:T(8,128)(2,1)}, u32[]{:S(2)}) copy-start(bf16[2048,8]{0,1:T(8,128)(2,1)} %param.16) | copy-start | bytes 98308
  6.5 50.9 %all-gather.9.cloned.1.call-start = ((), (), s32[]{:S(2)}) async-start(), calls=%async_computation.2 | async-start | bytes 1179648 | tf_op jit(solution)/shard_map/all_gather | solution.py:76
  7.3 87.1 %all-gather.13.cloned.1.call-start = ((), (), s32[]{:S(2)}) async-start(), calls=%async_computation.4 | async-start | bytes 2228224 | tf_op jit(solution)/shard_map/all_gather | solution.py:94
  8.0 149.0 %all-gather.11.cloned.1.call-start = ((), (), s32[]{:S(2)}) async-start(), calls=%async_computation.3 | async-start | bytes 8912896 | tf_op jit(solution)/shard_map/all_gather | solution.py:100
  8.7 221.3 %all-gather.7.cloned.1.call-start = ((), (), s32[]{:S(2)}) async-start(), calls=%async_computation.1 | async-start | bytes 13369344 | tf_op jit(solution)/shard_map/all_gather | solution.py:120
  9.3 351.6 %all-gather.15.cloned.1.call-start = ((), (), s32[]{:S(2)}) async-start(), calls=%async_computation.5 | async-start | bytes 4456448 | tf_op jit(solution)/shard_map/all_gather | solution.py:136
  59.0 39.6 %copy-start.3 = (s32[256,2]{0,1:T(2,128)S(1)}, s32[256,2]{0,1:T(2,128)}, u32[]{:S(2)}) copy-start(s32[256,2]{0,1:T(2,128)} %param.17) | copy-start | bytes 6148
  59.0 39.8 %copy-start.4 = (s32[4]{0:T(128)S(1)}, s32[4]{0:T(128)}, u32[]{:S(2)}) copy-start(s32[4]{0:T(128)} %param.22) | copy-start | bytes 52
  97.1 2.3 copy-start.5
  97.1 2.8 copy-start.1
  97.9 308.1 %all-gather.17.cloned.1.call-start = ((), (), s32[]{:S(2)}) async-start(), calls=%async_computation.6 | async-start | bytes 8912896 | tf_op jit(solution)/shard_map/all_gather | solution.py:153
  98.5 391.0 %reduce-scatter.2.cloned.1.call-start = ((), (), s32[]{:S(2)}) async-start(), calls=%async_computation.7 | async-start | bytes 2359296 | tf_op jit(solution)/shard_map/reduce_scatter | solution.py:156
  253.0 1.8 copy-start.2
  257.7 1.8 copy-start.2
  262.4 1.8 copy-start.2
  267.1 1.8 copy-start.2
  271.8 1.8 copy-start.2
  276.4 1.8 copy-start.2
  281.1 1.8 copy-start.2
  285.8 1.8 copy-start.2
  290.5 1.8 copy-start.2
  295.2 1.8 copy-start.2
  299.9 1.8 copy-start.2
  304.6 1.9 copy-start.2
  309.3 1.8 copy-start.2
  314.0 1.8 copy-start.2
  318.7 1.8 copy-start.2
  323.4 1.8 copy-start.2
  328.1 1.8 copy-start.2
  332.8 1.8 copy-start.2
  346.9 1.8 copy-start.2
  351.6 1.8 copy-start.2
  (4 other events, 7.1 us)
Sparse Core Ops, SparseCore 0:
  9.5 47.8 all-gather.8
  59.1 35.2 all-gather.12
  96.0 60.8 all-gather.10
  158.5 71.5 all-gather.6
  231.6 38.3 all-gather.14
  271.5 60.5 all-gather.16
  413.3 76.1 reduce-scatter.1
where the time goes:
time: 500 us; the launch traced here: 498 us
  waiting for transfers between devices  283 us (57%)
  matrix products  106 us (21%)
  local copies, waits for them, and re-layouts  68.3 us (14%)
  other arithmetic  24.2 us (5%)
  between operations  13.7 us (3%)
    reduce_scatter x1, waiting for transfers between devices, on_device(): lax.psum_scatter(partial_out, 'narrow', scatter_dimension=1, tiled=True)  76.3 us
    all_gather x1, waiting for transfers between devices, on_device(): shard_piece = lax.all_gather(prefix_cache, 'wide', axis=0, tiled=True)  65.7 us
    dot_general x32, matrix products, attend(): jnp.einsum('hrn,nhd->hrd', weights, value_block.astype(jnp.float32), prec...  62.4 us
    all_gather x1, waiting for transfers between devices, on_device(): lax.all_gather(query_weight, 'wide', axis=1, tiled=True)  55 us
    all_gather x1, waiting for transfers between devices, on_device(): whole = lax.all_gather(tokens, 'narrow', axis=1, tiled=True)  47.4 us
    dynamic_slice x80, local copies, waits for them, and re-layouts, over_blocks(): lax.scan(advance, carried, (cache_blocks, tenant_blocks, index_blocks))  37 us
    all_gather x1, waiting for transfers between devices, on_device(): lax.all_gather(kv_weight, 'wide', axis=1, tiled=True)  35.4 us
    dot_general x32, matrix products, attend(): jnp.einsum('hrd,nhd->hrn', queries, key_block, preferred_element_type=jnp...  25.4 us
  transfers between devices with their start and end apart: 7, of which 5 were waited for; matrix products, arithmetic and copies ran while one was open for 38% of the time, Pallas kernels for 0%

commit v1 on v0

--- a/solution.py
+++ b/solution.py
@@ -91,7 +91,9 @@
     choose = one_hot.astype(jnp.bfloat16)
     kv_part = lax.dot_general(
         normed,
-        lax.all_gather(kv_weight, "wide", axis=1, tiled=True),
+        jnp.concatenate(
+            lax.all_to_all(jnp.stack([kv_weight] * lax.axis_size("wide")), "wide", 0, 0), axis=1
+        ),
         (((1,), (1,)), ((), ())),
         preferred_element_type=jnp.float32,
     )

time: 500 us -> 464 us (0.928)
  waiting for transfers between devices: 283 us -> 240 us
  starting transfers between devices: 0.23 us -> 5.92 us
    all_gather x1 -> x0, waiting for transfers between devices: 35.4 us -> none  [on_device(): lax.all_gather(kv_weight, 'wide', axis=1, tiled=True)]
    all_to_all x0 -> x1, starting transfers between devices: none -> 5.72 us  [on_device(): lax.all_to_all(jnp.stack([kv_weight] * lax.axis_size('wide')), 'wide', 0, 0)]
  transfers between devices with their start and end apart: 7 -> 7, of which waited for: 5 -> 4; matrix products, arithmetic and copies ran while one was open for 38% -> 41% of each run, Pallas kernels for 0% -> 0%
where the time goes in v1:
time: 464 us; the launch traced here: 462 us
  waiting for transfers between devices  240 us (52%)
  matrix products  105 us (23%)
  local copies, waits for them, and re-layouts  70.8 us (15%)
  other arithmetic  23.5 us (5%)
  between operations  13.7 us (3%)
  starting transfers between devices  5.92 us (1%)
    reduce_scatter x1, waiting for transfers between devices, on_device(): lax.psum_scatter(partial_out, 'narrow', scatter_dimension=1, tiled=True)  76.3 us
    all_gather x1, waiting for transfers between devices, on_device(): shard_piece = lax.all_gather(prefix_cache, 'wide', axis=0, tiled=True)  65.8 us
    dot_general x32, matrix products, attend(): jnp.einsum('hrn,nhd->hrd', weights, value_block.astype(jnp.float32), prec...  62.4 us
    all_gather x1, waiting for transfers between devices, on_device(): lax.all_gather(query_weight, 'wide', axis=1, tiled=True)  52.7 us
    all_gather x1, waiting for transfers between devices, on_device(): whole = lax.all_gather(tokens, 'narrow', axis=1, tiled=True)  42.7 us
    dynamic_slice x80, local copies, waits for them, and re-layouts, over_blocks(): lax.scan(advance, carried, (cache_blocks, tenant_blocks, index_blocks))  37 us
    dot_general x32, matrix products, attend(): jnp.einsum('hrd,nhd->hrn', queries, key_block, preferred_element_type=jnp...  25.4 us
    another operation x1, local copies, waits for them, and re-layouts, over_blocks(): cache_rows.reshape((steps_count, block_size) + cache_rows.shape[1:])  18.1 us
  transfers between devices with their start and end apart: 7, of which 4 were waited for; matrix products, arithmetic and copies ran while one was open for 41% of the time, Pallas kernels for 0%

profile of v1, /device:TPU:0, one launch (start us, length us, event | category | flops | bytes accessed | tf_op | source)
XLA Modules:
  0.0 461.9 jit_solution(13415337850883714901)
XLA Ops:
  11.3 5.7 %all-to-all-start = ((bf16[16,512,128]{1,2,0:T(8,128)(2,1)}), bf16[16,512,128]{1,2,0:T(8,128)(2,1)S(1)}, u32[]{:S(2)}, u32[]{:S(2)}) async-start(bf16[16,512,128]{1,2,0:T(8,128)(2,1)} %stack.2), calls=%async_computation | async-start | bytes 4194304 | tf_op jit(solution)/shard_map/all_to_all | solution.py:95
  17.1 42.7 %all-gather.8.cloned.1.call-done = bf16[256,2048]{1,0:T(8,128)(2,1)} async-done(((bf16[256,256]{1,0:T(8,128)(2,1)}), bf16[256,2048]{1,0:T(8,128)(2,1)}) %all-gather.8.cloned.1.call-update) | async-done | bytes 1048592 | tf_op jit(solution)/shard_map/all_gather | solution.py:76
  61.3 2.0 convolution_convert_fusion.2
  68.2 52.7 %all-gather.10.cloned.1.call-done = bf16[2048,2048]{1,0:T(8,128)(2,1)} async-done(((bf16[2048,128]{1,0:T(8,128)(2,1)}), bf16[2048,2048]{1,0:T(8,128)(2,1)}) %all-gather.10.cloned.1.call-update) | async-done | bytes 8388624 | tf_op jit(solution)/shard_map/all_gather | solution.py:102
  120.8 5.8 %fusion.15 = bf16[32,8,16,128]{3,1,2,0:T(8,128)(2,1)S(1)} fusion(bf16[2048,2048]{1,0:T(8,128)(2,1)} %all-gather.10.cloned.1.call-done, bf16[256,2048]{1,0:T(8,128)(2,1)S(1)} %copy-done.2, f32[2048]{0:T(1024)S(1)} %convert_element_type.48, f32[256]{0:T(256)S(1)} %add_rsqrt_fusion), kind=kOutput, calls=%fused_computation.41 | convolution fusion | flops 2150105088 | bytes 10494976 | tf_op jit(solution)/shard_map/dot_general | solution.py:100
  128.3 65.8 %all-gather.6.cloned.1.call-done = bf16[12288,512]{1,0:T(8,128)(2,1)} async-done(((bf16[768,512]{1,0:T(8,128)(2,1)}), bf16[12288,512]{1,0:T(8,128)(2,1)}) %all-gather.6.cloned.1.call-update) | async-done | bytes 12582928 | tf_op jit(solution)/shard_map/all_gather | solution.py:122
  194.1 18.1 %reshape.243 = bf16[24,512,2,2,128]{4,3,2,1,0:T(2,128)(2,1)} reshape(bf16[12288,512]{1,0:T(8,128)(2,1)} %all-gather.6.cloned.1.call-done) | data formatting | bytes 25165824 | tf_op jit(solution)/shard_map/reshape;reshape | solution.py:44
  212.2 112.6 %while.31 = (s32[]{:T(128)}, f32[2,512]{1,0:T(2,128)S(1)}, f32[2,512]{1,0:T(2,128)S(1)}, f32[2,512,128]{2,1,0:T(8,128)S(1)}, s32[512]{0:T(512)S(1)}, /*index=5*/...) while((s32[]{:T(128)}, f32[2,512]{1,0:T(2,128)S(1)}, ...), condition=%wide.region_8.9_spmd.clone, body=%wide.region_5.8_spmd.clone.sunk | while | flops 943330304 | bytes 11870357 | solution.py:60
  214.9 2.0 fusion.61
  219.6 2.0 fusion.61
  224.3 2.0 fusion.61
  229.0 2.0 fusion.61
  233.7 2.0 fusion.61
  238.4 2.0 fusion.61
  243.1 2.0 fusion.61
  247.8 2.0 fusion.61
  252.5 2.0 fusion.61
  257.2 2.0 fusion.61
  261.9 2.0 fusion.61
  266.6 2.0 fusion.61
  271.3 2.0 fusion.61
  276.0 2.0 fusion.61
  280.7 2.0 fusion.61
  285.4 2.0 fusion.61
  290.1 2.0 fusion.61
  294.8 2.0 fusion.61
  299.5 2.0 fusion.61
  308.8 2.0 fusion.61
  318.2 2.0 fusion.61
  324.9 43.5 %while.30 = (s32[]{:T(128)}, f32[2,512]{1,0:T(2,128)S(1)}, f32[2,512]{1,0:T(2,128)S(1)}, f32[2,512,128]{2,1,0:T(8,128)S(1)}, s32[512]{0:T(512)S(1)}, /*index=5*/...) while((s32[]{:T(128)}, f32[2,512]{1,0:T(2,128)S(1)}, ...), condition=%wide.region_13.14_spmd.clone, body=%wide.region_10.13_spmd.clone.sunk | while | flops 943720448 | bytes 9789041 | solution.py:60
  370.0 7.1 %fusion.17 = f32[256,2048]{1,0:T(8,128)} fusion(bf16[2048,2048]{1,0:T(8,128)(2,1)} %all-gather.14.cloned.1.call-done, bf16[32,8,16,128]{3,2,1,0:T(8,128)(2,1)S(1)} %bitcast.101), kind=kOutput, calls=%fused_computation.45 | convolution fusion | flops 2147483648 | bytes 11534336 | tf_op jit(solution)/shard_map/dot_general | solution.py:153
  377.1 76.3 %reduce-scatter.2.cloned.1.call-done = f32[256,256]{1,0:T(8,128)} async-done(((f32[256,2048]{1,0:T(8,128)}), f32[256,256]{1,0:T(8,128)}) %reduce-scatter.2.cloned.1.call-update) | async-done | bytes 262160 | tf_op jit(solution)/shard_map/reduce_scatter | solution.py:158
  (417 shorter events, 128.2 us)
Async XLA Ops:
  6.5 59.6 %copy-start = (bf16[2048,8]{0,1:T(8,128)(2,1)S(1)}, bf16[2048,8]{0,1:T(8,128)(2,1)}, u32[]{:S(2)}) copy-start(bf16[2048,8]{0,1:T(8,128)(2,1)} %param.16) | copy-start | bytes 98308
  6.5 53.2 %all-gather.8.cloned.1.call-start = ((), (), s32[]{:S(2)}) async-start(), calls=%async_computation.3 | async-start | bytes 1179648 | tf_op jit(solution)/shard_map/all_gather | solution.py:76
  7.3 113.6 %all-gather.10.cloned.1.call-start = ((), (), s32[]{:S(2)}) async-start(), calls=%async_computation.4 | async-start | bytes 8912896 | tf_op jit(solution)/shard_map/all_gather | solution.py:102
  8.0 186.1 %all-gather.6.cloned.1.call-start = ((), (), s32[]{:S(2)}) async-start(), calls=%async_computation.2 | async-start | bytes 13369344 | tf_op jit(solution)/shard_map/all_gather | solution.py:122
  11.3 5.8 %copy-start.4 = (bf16[2048]{0:T(1024)(128)(2,1)S(1)}, bf16[2048]{0:T(1024)(128)(2,1)}, u32[]{:S(2)}) copy-start(bf16[2048]{0:T(1024)(128)(2,1)} %param.15) | copy-start | bytes 12292
  11.3 50.0 %all-to-all-start = ((bf16[16,512,128]{1,2,0:T(8,128)(2,1)}), bf16[16,512,128]{1,2,0:T(8,128)(2,1)S(1)}, u32[]{:S(2)}, u32[]{:S(2)}) async-start(bf16[16,512,128]{1,2,0:T(8,128)(2,1)} %stack.2), calls=%async_computation | async-start | bytes 4194304 | tf_op jit(solution)/shard_map/all_to_all | solution.py:95
  17.0 307.9 %all-gather.12.cloned.1.call-start = ((), (), s32[]{:S(2)}) async-start(), calls=%async_computation.5 | async-start | bytes 4456448 | tf_op jit(solution)/shard_map/all_gather | solution.py:138
  61.3 3.6 copy-start.5
  61.3 3.7 copy-start.6
  63.3 2.3 copy-start.7
  63.3 2.8 copy-start.2
  64.2 305.8 %all-gather.14.cloned.1.call-start = ((), (), s32[]{:S(2)}) async-start(), calls=%async_computation.6 | async-start | bytes 8912896 | tf_op jit(solution)/shard_map/all_gather | solution.py:155
  64.8 388.6 %reduce-scatter.2.cloned.1.call-start = ((), (), s32[]{:S(2)}) async-start(), calls=%async_computation.7 | async-start | bytes 2359296 | tf_op jit(solution)/shard_map/reduce_scatter | solution.py:158
  216.9 1.8 copy-start.3
  221.6 1.8 copy-start.3
  226.3 1.8 copy-start.3
  231.0 1.8 copy-start.3
  235.7 1.8 copy-start.3
  245.1 1.8 copy-start.3
  249.8 1.8 copy-start.3
  254.5 1.8 copy-start.3
  259.2 1.8 copy-start.3
  268.5 1.9 copy-start.3
  273.3 1.8 copy-start.3
  278.0 1.8 copy-start.3
  282.7 1.8 copy-start.3
  287.4 1.8 copy-start.3
  292.1 1.8 copy-start.3
  296.8 1.8 copy-start.3
  315.5 1.8 copy-start.3
  320.2 1.8 copy-start.3
  370.0 85.0 %copy-start.1 = (bf16[2048,8]{0,1:T(8,128)(2,1)S(1)}, bf16[2048,8]{0,1:T(8,128)(2,1)}, u32[]{:S(2)}) copy-start(bf16[2048,8]{0,1:T(8,128)(2,1)} %param.16) | copy-start | bytes 98308
  (6 other events, 10.7 us)
Sparse Core Ops, SparseCore 0:
  9.5 50.1 all-gather.7
  61.4 59.3 all-gather.9
  122.5 71.5 all-gather.5
  195.6 38.3 all-gather.11
  235.5 60.5 all-gather.13
  377.3 76.1 reduce-scatter.1
